TPU v7x, 256 devices: a whole 4x4x8 slice. The times are simulated.
256 devices in a mesh: row: 32 (over y, z), col: 8 (over x, core).
Axes of the slice: x: 4, y: 4, z: 8, core: 2. Of those that a mesh axis runs over, the one named last changes fastest.
Arguments:
- diag_block: float32 [256, 256], P(('row', 'col')), may hold values from -1 to 40, as said below
- panel: float32 [24576, 256], P(('row', 'col')), may hold values from -6 to 6
- trailing: bfloat16 [24576, 24576], P('row', 'col'), may hold values from -6 to 6
Outputs:
- diag_factor: float32 [256, 256], P(('row', 'col'))
- panel_factor: float32 [24576, 256], P(('row', 'col'))
- trailing_out: bfloat16 [24576, 24576], P('row', 'col')
Inputs may be any that keep to these rules, and one draw needn't show every extreme that they name: diag_block is symmetric, with off-diagonal entries in -1 to 1 and diagonal entries in 24 to 40, so it is positive definite.
All inputs are finite; a program needn't handle non-finite values.
Results may differ from a plain program's by a relative error of at most 0.001.
Values sent between devices are 32-bit elements; how exact they have to be, the bound alone decides.
No kernel may reach another device: no remote copies, remote signals or barrier semaphores. Data moves between devices by JAX's collectives and lax.ppermute only.
A program may use at most 128 MiB of HBM per device.

v0:
```python
import jax
import jax.numpy as jnp
from jax import lax
from jax.sharding import PartitionSpec as P

BLOCK = 256
GRID = ("row", "col")
HIGHEST = lax.Precision.HIGHEST
HIGH = lax.Precision.HIGH


def product(a, b, precision=HIGHEST):
    return jnp.dot(a, b, precision=precision, preferred_element_type=jnp.float32)


def per_device(diag_block, panel, trailing):
    count_rows, count_cols = (lax.axis_size("row"), lax.axis_size("col"))
    devices = count_rows * count_cols
    ratio = count_rows // count_cols
    panel_width = panel.shape[1]
    swap = [
        ((r * count_cols + a) * count_cols + b, (r * count_cols + b) * count_cols + a)
        for r in range(ratio)
        for a in range(count_cols)
        for b in range(count_cols)
    ]
    moved = lax.ppermute(panel, GRID, swap)
    column_rows = lax.all_gather(moved, "row", axis=0, tiled=True)
    diag_share = diag_block.shape[0]
    copies = jnp.broadcast_to(diag_block[None], (devices,) + diag_block.shape)
    copies = copies.reshape(devices * diag_share, panel_width)
    whole_diag = lax.all_to_all(copies, GRID, 0, 0, tiled=True)
    row_rows = lax.all_gather(panel, "col", axis=0, tiled=True)
    diag_factor = jnp.linalg.cholesky(whole_diag)
    identity = jnp.eye(panel_width, dtype=jnp.float32)
    inverse = lax.linalg.triangular_solve(diag_factor, identity, left_side=True, lower=True)
    panel_factor = product(panel, inverse.T)
    factor_rows = lax.dynamic_slice_in_dim(
        diag_factor, lax.axis_index(GRID) * diag_share, diag_share, 0
    )
    left = product(product(row_rows, inverse.T), inverse)
    per_block = row_rows.shape[0] // BLOCK
    grouped = column_rows.reshape(ratio, per_block, BLOCK, panel_width)
    right = jnp.transpose(grouped, (1, 0, 2, 3)).reshape(-1, panel_width)
    update = product(left, right.T, HIGH)
    trailing_out = (trailing.astype(jnp.float32) - update).astype(jnp.bfloat16)
    return (factor_rows, panel_factor, trailing_out)


def solution(mesh):
    placed = (P(GRID, None), P(GRID, None), P("row", "col"))
    return jax.shard_map(per_device, mesh=mesh, in_specs=placed, out_specs=placed, check_vma=False)
```

profile of v0, /device:TPU:1, one launch (start us, length us, event | category | flops | bytes accessed | tf_op | source)
XLA Modules:
  0.0 135.2 jit_solution(17759163634431748561)
XLA Ops:
  7.2 0.0 copy-start
  7.2 0.0 all-gather.2.cloned.1.call-start
  7.2 4.9 %collective-permute-start = (f32[96,256]{1,0:T(8,128)}, f32[96,256]{1,0:T(8,128)S(1)}, u32[]{:S(2)}, u32[]{:S(2)}) collective-permute-start(f32[96,256]{1,0:T(8,128)} %param.4), channel_id=1, source_target_pairs={{0,0},{1,8},{2,16},{3,24},{4,32},{5,40},{6,48},{7,56},{8,1},{9,9},... | collective-permute-start | bytes 294920 | tf_op jit(solution)/shard_map/ppermute | solution.py:27
  12.2 2.5 %collective-permute-done = f32[96,256]{1,0:T(8,128)S(1)} collective-permute-done((f32[96,256]{1,0:T(8,128)}, f32[96,256]{1,0:T(8,128)S(1)}, u32[]{:S(2)}, u32[]{:S(2)}) %collective-permute-start) | collective-permute-done | bytes 98336 | tf_op jit(solution)/shard_map/ppermute | solution.py:27
  14.7 0.0 copy-start.1
  14.7 0.6 copy-done.1
  15.3 0.0 all-gather.2.cloned.1.call-update
  15.3 1.5 %reshape.41 = f32[256,1,256]{2,1,0:T(1,128)} broadcast(f32[256]{0:T(256)} %bitcast.49), dimensions={2} | broadcast | bytes 263168 | tf_op jit(solution)/shard_map/reshape | solution.py:31
  16.8 20.7 %all-to-all-start = ((f32[256,1,256]{2,1,0:T(1,128)}), f32[256,1,256]{2,1,0:T(1,128)S(1)}, u32[]{:S(2)}, u32[]{:S(2)}) async-start(f32[256,1,256]{2,1,0:T(1,128)} %reshape.41), calls=%async_computation | async-start | bytes 524288 | tf_op jit(solution)/shard_map/all_to_all | solution.py:32
  37.6 16.0 %all_gather.6 = f32[768,256]{1,0:T(8,128)S(1)} all-gather(f32[96,256]{1,0:T(8,128)} %param.4), channel_id=1, replica_groups=mesh['row'=32,'col'=8] {'col'}, dimensions={0}, use_global_device_ids=true | all-gather | bytes 884736 | tf_op jit(solution)/shard_map/all_gather | solution.py:33
  53.6 0.5 all-to-all-done
  54.1 0.1 copy.10
  54.3 11.7 %cholesky.50 = f32[128,128]{1,0:T(8,128)S(1)} custom-call(f32[128,128]{1,0:T(8,128)S(1)} %cholesky.118), custom_call_target="Cholesky" | custom-call | tf_op jit(solution)/shard_map/jit(cholesky)/cholesky | solution.py:34
  66.1 9.8 %custom-call.14 = f32[1,128,128]{1,2,0:T(8,128)S(1)} custom-call(f32[1,128,128]{2,1,0:T(8,128)S(1)} %get-tuple-element.26), custom_call_target="InvertDiagBlocksLowerTriangular" | custom-call | tf_op jit(solution)/shard_map/jit(cholesky)/cholesky | solution.py:34
  75.9 0.2 constant_dynamic-update-slice_fusion
  76.1 0.3 convolution_subtract_fusion.1
  76.4 11.7 %cholesky.105 = f32[128,128]{1,0:T(8,128)S(1)} custom-call(f32[128,128]{1,0:T(8,128)S(1)} %convolution_subtract_fusion.1), custom_call_target="Cholesky" | custom-call | tf_op jit(solution)/shard_map/jit(cholesky)/cholesky | solution.py:34
  88.1 0.6 compare_reduce_fusion
  90.1 0.1 triangular_solve.44
  90.2 4.1 %while.1 = (s32[]{:T(128)}, f32[256,256]{1,0:T(8,128)S(1)}, s32[2,2]{1,0:T(2,128)S(1)}, f32[2,128,128]{2,1,0:T(8,128)S(1)}, s32[]{:T(128)}) while((s32[]{:T(128)}, f32[256,256]{1,0:T(8,128)S(1)}, s32[2,2]{1,0:T(2,128)S(1)}, f32[2,128,128]{2,1,0:T(8,128)S(1)}, s32[]{:T(128)}) %tuple.28), condition=%wide.while_cond, body=%wide.while_body.sunk | while | flops 2 | bytes 131189 | solution.py:36
  90.3 0.6 fusion.25
  90.9 1.4 %bitcast_dynamic-update-slice_fusion.2 = f32[2,128,128]{2,1,0:T(8,128)S(1)} fusion(f32[2,128,128]{2,1,0:T(8,128)S(1)} %get-tuple-element.68, s32[]{:T(128)S(6)} %copy.20, f32[256,256]{1,0:T(8,128)S(1)} %get-tuple-element.71, s32[]{:T(128)} %bitcast.45, s32[]{:T(128)} %bitcast.46), kind=kLoop, calls=%fused_computation.clone.1 | loop fusion | bytes 131084 | tf_op jit(solution)/shard_map/triangular_solve
  92.3 0.6 fusion.25
  92.9 1.4 %bitcast_dynamic-update-slice_fusion.2 = f32[2,128,128]{2,1,0:T(8,128)S(1)} fusion(f32[2,128,128]{2,1,0:T(8,128)S(1)} %get-tuple-element.68, s32[]{:T(128)S(6)} %copy.20, f32[256,256]{1,0:T(8,128)S(1)} %get-tuple-element.71, s32[]{:T(128)} %bitcast.45, s32[]{:T(128)} %bitcast.46), kind=kLoop, calls=%fused_computation.clone.1 | loop fusion | bytes 131084 | tf_op jit(solution)/shard_map/triangular_solve
  94.3 19.7 %custom-call.15 = f32[2,128,128]{1,2,0:T(8,128)S(1)} custom-call(f32[2,128,128]{2,1,0:T(8,128)S(1)} %get-tuple-element.10), custom_call_target="InvertDiagBlocksLowerTriangular" | custom-call | tf_op jit(solution)/shard_map/triangular_solve | solution.py:36
  114.0 0.6 constant_dynamic-slice_fusion.1
  114.6 0.3 fusion.4
  114.9 0.3 convolution_subtract_fusion
  115.1 0.3 fusion.7
  115.4 0.0 copy-done
  115.4 1.0 convolution_bitcast_fusion
  116.5 0.8 fusion.3
  117.3 1.4 %fusion.2 = f32[768,256]{1,0:T(8,128)S(1)} fusion(f32[256,768]{1,0:T(8,128)S(1)} %fusion.3, f32[128,256]{1,0:T(8,128)S(1)} %fusion.7, f32[128,256]{1,0:T(8,128)S(1)} %fusion.4), kind=kOutput, calls=%fused_computation.13 | convolution fusion | flops 604045312 | bytes 1835008 | tf_op jit(solution)/shard_map/dot_general | solution.py:13
  118.8 0.0 all-gather.2.cloned.1.call-done
  118.8 2.1 %copy.12 = f32[3,4,256,256]{3,2,1,0:T(8,128)S(1)} copy(f32[3,4,256,256]{3,2,0,1:T(8,128)} %bitcast.48) | data formatting | bytes 6291456 | tf_op jit(solution)/shard_map/transpose | solution.py:44
  120.9 7.5 %subtract_convert_fusion = bf16[768,3072]{1,0:T(8,128)(2,1)} fusion(bf16[768,3072]{1,0:T(8,128)(2,1)} %param.5, f32[768,256]{1,0:T(8,128)S(1)} %fusion.2, f32[3072,256]{1,0:T(8,128)S(1)} %bitcast.47), kind=kOutput, calls=%fused_computation.2 | convolution fusion | flops 3630956544 | bytes 13369344 | tf_op jit(solution)/shard_map/dot_general | solution.py:13
  (11 shorter events, 0.2 us)
Async XLA Ops:
  7.2 108.3 %copy-start = (f32[96,256]{1,0:T(8,128)S(1)}, f32[96,256]{1,0:T(8,128)}, u32[]{:S(2)}) copy-start(f32[96,256]{1,0:T(8,128)} %param.4) | copy-start | bytes 294916
  7.2 111.6 %all-gather.2.cloned.1.call-start = ((), (), s32[]{:S(2)}) async-start(), calls=%async_computation.1 | async-start | bytes 3244032 | tf_op jit(solution)/shard_map/all_gather | solution.py:28
  7.2 7.4 %collective-permute-start = (f32[96,256]{1,0:T(8,128)}, f32[96,256]{1,0:T(8,128)S(1)}, u32[]{:S(2)}, u32[]{:S(2)}) collective-permute-start(f32[96,256]{1,0:T(8,128)} %param.4), channel_id=1, source_target_pairs={{0,0},{1,8},{2,16},{3,24},{4,32},{5,40},{6,48},{7,56},{8,1},{9,9},... | collective-permute-start | bytes 294920 | tf_op jit(solution)/shard_map/ppermute | solution.py:27
  14.7 0.6 copy-start.1
  16.8 37.3 %all-to-all-start = ((f32[256,1,256]{2,1,0:T(1,128)}), f32[256,1,256]{2,1,0:T(1,128)S(1)}, u32[]{:S(2)}, u32[]{:S(2)}) async-start(f32[256,1,256]{2,1,0:T(1,128)} %reshape.41), calls=%async_computation | async-start | bytes 524288 | tf_op jit(solution)/shard_map/all_to_all | solution.py:32
Sparse Core Ops, SparseCore 0:
  15.4 85.1 all-gather.1
where the time goes:
time: 136 us; the launch traced here: 135 us
  other arithmetic  53.7 us (39%)
  starting transfers between devices  25.7 us (19%)
  blocking collectives  16 us (12%)
  between operations  15.5 us (11%)
  matrix products  12.1 us (9%)
  local copies, waits for them, and re-layouts  9.01 us (7%)
  waiting for transfers between devices  3.02 us (2%)
    another operation x6, other arithmetic, per_device(): diag_factor = jnp.linalg.cholesky(whole_diag)  34 us
    all_to_all x1, starting transfers between devices, per_device(): whole_diag = lax.all_to_all(copies, GRID, 0, 0, tiled=True)  20.7 us
    another operation x3, other arithmetic, per_device(): lax.linalg.triangular_solve(diag_factor, identity, left_side=True, lower=...  19.7 us
    all_gather x1, blocking collectives, per_device(): row_rows = lax.all_gather(panel, 'col', axis=0, tiled=True)  16 us
    dot_general x4, matrix products, product(): jnp.dot(a, b, precision=precision, preferred_element_type=jnp.float32)  10.8 us
    ppermute x1, starting transfers between devices, per_device(): moved = lax.ppermute(panel, GRID, swap)  4.93 us
    another operation x6, local copies, waits for them, and re-layouts  3.95 us
  transfers between devices with their start and end apart: 3, of which 2 were waited for; matrix products, arithmetic and copies ran while one was open for 48% of the time, Pallas kernels for 0%

commit v1 on v0

--- a/solution.py
+++ b/solution.py
@@ -30,7 +30,9 @@
     copies = jnp.broadcast_to(diag_block[None], (devices,) + diag_block.shape)
     copies = copies.reshape(devices * diag_share, panel_width)
     whole_diag = lax.all_to_all(copies, GRID, 0, 0, tiled=True)
-    row_rows = lax.all_gather(panel, "col", axis=0, tiled=True)
+    row_rows = jnp.concatenate(
+        lax.all_to_all(jnp.stack([panel] * lax.axis_size("col")), "col", 0, 0), axis=0
+    )
     diag_factor = jnp.linalg.cholesky(whole_diag)
     identity = jnp.eye(panel_width, dtype=jnp.float32)
     inverse = lax.linalg.triangular_solve(diag_factor, identity, left_side=True, lower=True)

time: 136 us -> 141 us (1.037)
  blocking collectives: 16 us -> 0 us
  waiting for transfers between devices: 3.02 us -> 19 us
  starting transfers between devices: 25.7 us -> 29.5 us
  local copies, waits for them, and re-layouts: 9.01 us -> 10.9 us
    all_to_all x1, waiting for transfers between devices: 0.49 us -> 16.5 us  [per_device(): whole_diag = lax.all_to_all(copies, GRID, 0, 0, tiled=True)]
    all_gather x1 -> x0, blocking collectives: 16 us -> none  [per_device(): row_rows = lax.all_gather(panel, 'col', axis=0, tiled=True)]
    all_to_all x0 -> x1, starting transfers between devices: none -> 3.82 us  [per_device(): lax.all_to_all(jnp.stack([panel] * lax.axis_size('col')), 'col', 0, 0)]
    another operation x6 -> x7, local copies, waits for them, and re-layouts: 3.95 us -> 5.8 us
  transfers between devices with their start and end apart: 3 -> 4, of which waited for: 2 -> 2; matrix products, arithmetic and copies ran while one was open for 48% -> 47% of each run, Pallas kernels for 0% -> 0%
where the time goes in v1:
time: 141 us
  other arithmetic  53.9 us (38%)
  starting transfers between devices  29.5 us (21%)
  waiting for transfers between devices  19 us (13%)
  between operations  15.5 us (11%)
  matrix products  12.1 us (9%)
  local copies, waits for them, and re-layouts  10.9 us (8%)
    another operation x6, other arithmetic, per_device(): diag_factor = jnp.linalg.cholesky(whole_diag)  34 us
    all_to_all x1, starting transfers between devices, per_device(): whole_diag = lax.all_to_all(copies, GRID, 0, 0, tiled=True)  20.7 us
    another operation x3, other arithmetic, per_device(): lax.linalg.triangular_solve(diag_factor, identity, left_side=True, lower=...  19.9 us
    all_to_all x1, waiting for transfers between devices, per_device(): whole_diag = lax.all_to_all(copies, GRID, 0, 0, tiled=True)  16.5 us
    dot_general x4, matrix products, product(): jnp.dot(a, b, precision=precision, preferred_element_type=jnp.float32)  10.8 us
    ppermute x1, starting transfers between devices, per_device(): moved = lax.ppermute(panel, GRID, swap)  4.93 us
    another operation x6, local copies, waits for them, and re-layouts  3.96 us
    all_to_all x1, starting transfers between devices, per_device(): lax.all_to_all(jnp.stack([panel] * lax.axis_size('col')), 'col', 0, 0)  3.82 us
  transfers between devices with their start and end apart: 4, of which 2 were waited for; matrix products, arithmetic and copies ran while one was open for 47% of the time, Pallas kernels for 0%

profile of v1, /device:TPU:1, one launch (start us, length us, event | category | flops | bytes accessed | tf_op | source)
XLA Modules:
  0.0 140.9 jit_solution(3135027421657996628)
XLA Ops:
  7.2 0.0 copy-start
  7.2 0.0 all-gather.2.cloned.1.call-start
  7.2 4.9 %collective-permute-start = (f32[96,256]{1,0:T(8,128)}, f32[96,256]{1,0:T(8,128)S(1)}, u32[]{:S(2)}, u32[]{:S(2)}) collective-permute-start(f32[96,256]{1,0:T(8,128)} %param.4), channel_id=1, source_target_pairs={{0,0},{1,8},{2,16},{3,24},{4,32},{5,40},{6,48},{7,56},{8,1},{9,9},... | collective-permute-start | bytes 294920 | tf_op jit(solution)/shard_map/ppermute | solution.py:27
  12.2 2.5 %collective-permute-done = f32[96,256]{1,0:T(8,128)S(1)} collective-permute-done((f32[96,256]{1,0:T(8,128)}, f32[96,256]{1,0:T(8,128)S(1)}, u32[]{:S(2)}, u32[]{:S(2)}) %collective-permute-start) | collective-permute-done | bytes 98336 | tf_op jit(solution)/shard_map/ppermute | solution.py:27
  14.7 0.0 copy-start.1
  14.7 0.6 copy-done.1
  15.3 0.0 all-gather.2.cloned.1.call-update
  15.3 1.5 %reshape.46 = f32[256,1,256]{2,1,0:T(1,128)} broadcast(f32[256]{0:T(256)} %bitcast.51), dimensions={2} | broadcast | bytes 263168 | tf_op jit(solution)/shard_map/reshape | solution.py:31
  16.8 20.7 %all-to-all-start = ((f32[256,1,256]{2,1,0:T(1,128)}), f32[256,1,256]{2,1,0:T(1,128)S(1)}, u32[]{:S(2)}, u32[]{:S(2)}) async-start(f32[256,1,256]{2,1,0:T(1,128)} %reshape.46), calls=%async_computation | async-start | bytes 524288 | tf_op jit(solution)/shard_map/all_to_all | solution.py:32
  37.6 16.5 %all-to-all-done = f32[256,1,256]{2,1,0:T(1,128)S(1)} async-done(((f32[256,1,256]{2,1,0:T(1,128)}), f32[256,1,256]{2,1,0:T(1,128)S(1)}, u32[]{:S(2)}, u32[]{:S(2)}) %all-to-all-start) | async-done | bytes 262176 | tf_op jit(solution)/shard_map/all_to_all | solution.py:32
  54.1 1.8 %stack.2 = f32[8,96,256]{2,1,0:T(8,128)} broadcast(f32[96,256]{1,0:T(8,128)} %param.4), dimensions={1,2} | broadcast | bytes 884736 | tf_op jit(solution)/shard_map/stack | solution.py:34
  55.9 3.8 %all-to-all-start.1 = ((f32[8,96,256]{2,1,0:T(8,128)}), f32[8,96,256]{2,1,0:T(8,128)S(1)}, u32[]{:S(2)}, u32[]{:S(2)}) async-start(f32[8,96,256]{2,1,0:T(8,128)} %stack.2), calls=%async_computation.1 | async-start | bytes 1572864 | tf_op jit(solution)/shard_map/all_to_all | solution.py:34
  59.8 0.1 copy.10
  60.0 11.7 %cholesky.50 = f32[128,128]{1,0:T(8,128)S(1)} custom-call(f32[128,128]{1,0:T(8,128)S(1)} %cholesky.118), custom_call_target="Cholesky" | custom-call | tf_op jit(solution)/shard_map/jit(cholesky)/cholesky | solution.py:36
  71.7 9.8 %custom-call.14 = f32[1,128,128]{1,2,0:T(8,128)S(1)} custom-call(f32[1,128,128]{2,1,0:T(8,128)S(1)} %get-tuple-element.26), custom_call_target="InvertDiagBlocksLowerTriangular" | custom-call | tf_op jit(solution)/shard_map/jit(cholesky)/cholesky | solution.py:36
  81.6 0.2 constant_dynamic-update-slice_fusion
  81.8 0.3 convolution_subtract_fusion.1
  82.0 11.7 %cholesky.105 = f32[128,128]{1,0:T(8,128)S(1)} custom-call(f32[128,128]{1,0:T(8,128)S(1)} %convolution_subtract_fusion.1), custom_call_target="Cholesky" | custom-call | tf_op jit(solution)/shard_map/jit(cholesky)/cholesky | solution.py:36
  93.8 0.6 compare_reduce_fusion
  95.8 0.1 triangular_solve.44
  95.9 4.0 %while.1 = (s32[]{:T(128)}, f32[256,256]{1,0:T(8,128)S(1)}, s32[2,2]{1,0:T(2,128)S(1)}, f32[2,128,128]{2,1,0:T(8,128)S(1)}, s32[]{:T(128)}) while((s32[]{:T(128)}, f32[256,256]{1,0:T(8,128)S(1)}, s32[2,2]{1,0:T(2,128)S(1)}, f32[2,128,128]{2,1,0:T(8,128)S(1)}, s32[]{:T(128)}) %tuple.28), condition=%wide.while_cond, body=%wide.while_body.sunk | while | flops 2 | bytes 131189 | solution.py:38
  95.9 0.6 fusion.25
  96.4 1.4 bitcast_dynamic-update-slice_fusion.2
  97.9 0.6 fusion.25
  98.5 1.4 bitcast_dynamic-update-slice_fusion.2
  99.8 19.9 %custom-call.15 = f32[2,128,128]{1,2,0:T(8,128)S(1)} custom-call(f32[2,128,128]{2,1,0:T(8,128)S(1)} %get-tuple-element.10), custom_call_target="InvertDiagBlocksLowerTriangular" | custom-call | tf_op jit(solution)/shard_map/triangular_solve | solution.py:38
  119.7 0.6 constant_dynamic-slice_fusion.1
  120.3 0.3 fusion.4
  120.6 0.3 convolution_subtract_fusion
  120.8 0.3 fusion.7
  121.1 0.0 copy-done
  121.2 1.0 convolution_bitcast_fusion
  122.2 0.0 all-to-all-done.1
  122.2 0.8 fusion.3
  123.0 1.4 %fusion.2 = f32[768,256]{1,0:T(8,128)S(1)} fusion(f32[256,768]{1,0:T(8,128)S(1)} %fusion.3, f32[128,256]{1,0:T(8,128)S(1)} %fusion.7, f32[128,256]{1,0:T(8,128)S(1)} %fusion.4), kind=kOutput, calls=%fused_computation.13 | convolution fusion | flops 604045312 | bytes 1835008 | tf_op jit(solution)/shard_map/dot_general | solution.py:13
  124.5 0.0 all-gather.2.cloned.1.call-done
  124.5 2.1 %copy.12 = f32[3,4,256,256]{3,2,1,0:T(8,128)S(1)} copy(f32[3,4,256,256]{3,2,0,1:T(8,128)} %bitcast.50) | data formatting | bytes 6291456 | tf_op jit(solution)/shard_map/transpose | solution.py:46
  126.6 7.5 %subtract_convert_fusion = bf16[768,3072]{1,0:T(8,128)(2,1)} fusion(bf16[768,3072]{1,0:T(8,128)(2,1)} %param.5, f32[768,256]{1,0:T(8,128)S(1)} %fusion.2, f32[3072,256]{1,0:T(8,128)S(1)} %bitcast.48), kind=kOutput, calls=%fused_computation.2 | convolution fusion | flops 3630956544 | bytes 13369344 | tf_op jit(solution)/shard_map/dot_general | solution.py:13
  (11 shorter events, 0.2 us)
Async XLA Ops:
  7.2 114.0 %copy-start = (f32[96,256]{1,0:T(8,128)S(1)}, f32[96,256]{1,0:T(8,128)}, u32[]{:S(2)}) copy-start(f32[96,256]{1,0:T(8,128)} %param.4) | copy-start | bytes 294916
  7.2 117.3 %all-gather.2.cloned.1.call-start = ((), (), s32[]{:S(2)}) async-start(), calls=%async_computation.2 | async-start | bytes 3244032 | tf_op jit(solution)/shard_map/all_gather | solution.py:28
  7.2 7.4 %collective-permute-start = (f32[96,256]{1,0:T(8,128)}, f32[96,256]{1,0:T(8,128)S(1)}, u32[]{:S(2)}, u32[]{:S(2)}) collective-permute-start(f32[96,256]{1,0:T(8,128)} %param.4), channel_id=1, source_target_pairs={{0,0},{1,8},{2,16},{3,24},{4,32},{5,40},{6,48},{7,56},{8,1},{9,9},... | collective-permute-start | bytes 294920 | tf_op jit(solution)/shard_map/ppermute | solution.py:27
  14.7 0.6 copy-start.1
  16.8 37.3 %all-to-all-start = ((f32[256,1,256]{2,1,0:T(1,128)}), f32[256,1,256]{2,1,0:T(1,128)S(1)}, u32[]{:S(2)}, u32[]{:S(2)}) async-start(f32[256,1,256]{2,1,0:T(1,128)} %reshape.46), calls=%async_computation | async-start | bytes 524288 | tf_op jit(solution)/shard_map/all_to_all | solution.py:32
  55.9 66.2 %all-to-all-start.1 = ((f32[8,96,256]{2,1,0:T(8,128)}), f32[8,96,256]{2,1,0:T(8,128)S(1)}, u32[]{:S(2)}, u32[]{:S(2)}) async-start(f32[8,96,256]{2,1,0:T(8,128)} %stack.2), calls=%async_computation.1 | async-start | bytes 1572864 | tf_op jit(solution)/shard_map/all_to_all | solution.py:34
Sparse Core Ops, SparseCore 0:
  15.4 84.9 all-gather.1
